TPU v7x, 256 devices: a whole 4x4x8 slice. The times are simulated.
256 devices in a mesh: line: 8 (over z_hi, core), dp: 32 (over z_lo, x, y).
Axes of the slice: x: 4, y: 4, z: 8 (z_hi: 4, z_lo: 2; z = z_hi * 2 + z_lo), core: 2. Of those that a mesh axis runs over, the one named last changes fastest.
Arguments:
- fields: bfloat16 [32, 4096, 128], P('dp', 'line'), may hold values from -6 to 6
- cotangent: bfloat16 [32, 4096, 128], P('dp', 'line'), may hold values from -6 to 6
- norm_gain: float32 [3, 128], replicated, may hold values from 0.1 to 1.9
- kernel: float32 [3, 15, 128], replicated, may hold values from -1.8 to 1.8
- mix_weight: bfloat16 [3, 128, 128], replicated, may hold values from -0.5 to 0.5
- line_order: int32 [3, 4096], P(None, 'line'), may hold values from 0 to 511, as said below
- line_starts: int32 [3, 32], P(None, 'line'), may hold values from 0 to 32
Outputs:
- imitated: bfloat16 [32, 4096, 128], P('dp', 'line')
- field_grad: bfloat16 [32, 4096, 128], P('dp', 'line')
- mix_grad: float32 [3, 128, 128], replicated
- kernel_grad: float32 [3, 15, 128], replicated
- gain_grad: float32 [3, 128], replicated
Inputs may be any that keep to these rules, and one draw needn't show every extreme that they name: For each direction, every aligned block of 512 entries of line_order is a permutation of 0 to 511.
All inputs are finite; a program needn't handle non-finite values.
Results may differ from a plain program's by a relative error of at most 0.014.
Values may be sent and summed in bfloat16 or wider, within the bound.
No kernel may reach another device: no remote copies, remote signals or barrier semaphores. Data moves between devices by JAX's collectives and lax.ppermute only.
A program may use at most 64 MiB of HBM per device.

v0:
```python
import jax
import jax.numpy as jnp
from jax import lax
from jax.sharding import PartitionSpec as P

LINE = 128
EPSILON = 1e-06


def tap_offsets():
    offsets = [0]
    for dilation_level in range(7):
        offsets = offsets + [-(2**dilation_level), 2**dilation_level]
    return offsets


def shifted(values, offset):
    if offset > 0:
        return jnp.concatenate([values[:, offset:], jnp.zeros_like(values[:, :offset])], axis=1)
    if offset < 0:
        return jnp.concatenate([jnp.zeros_like(values[:, offset:]), values[:, :offset]], axis=1)
    return values


def depthwise(inputs, weights):
    running = jnp.zeros(inputs.shape, jnp.float32)
    for tap_index, offset in enumerate(tap_offsets()):
        running = running + weights[tap_index] * shifted(inputs, offset)
    return running


def depthwise_transpose(grads, weights):
    running = jnp.zeros(grads.shape, jnp.float32)
    for tap_index, offset in enumerate(tap_offsets()):
        running = running + weights[tap_index] * shifted(grads, -offset)
    return running


def kernel_terms(grads, inputs):
    return jnp.stack(
        [jnp.sum(grads * shifted(inputs, offset), axis=(0, 1)) for offset in tap_offsets()]
    )


def block_view(array, line_count):
    batch_len, cell_count, channels = array.shape
    return array.reshape(batch_len, line_count, cell_count // line_count, channels)


def unpermute(array, table):
    return jnp.zeros_like(array).at[:, table].set(array)


def into_lines(array, table, shift, line_count):
    rolled = jnp.roll(block_view(array, line_count), shift, axis=1).reshape(array.shape)
    received = lax.all_to_all(rolled, "line", split_axis=1, concat_axis=1, tiled=True)
    return jnp.take(received, table, axis=1)


def out_of_lines(array, table, shift, line_count):
    placed = unpermute(array, table)
    received = lax.all_to_all(placed, "line", split_axis=1, concat_axis=1, tiled=True)
    return jnp.roll(block_view(received, line_count), -shift, axis=1).reshape(array.shape)


def norm_forward(stream, gain_row):
    values = stream.astype(jnp.float32)
    inverse = lax.rsqrt(jnp.mean(values * values, axis=-1, keepdims=True) + EPSILON)
    scaled = values * inverse
    normed = (scaled * gain_row).astype(jnp.bfloat16)
    return (values, inverse, scaled, normed)


def norm_backward(grad_cells, inverse, scaled, gain_row, grad_stream):
    cells_f = grad_cells.astype(jnp.float32)
    gain_part = jnp.sum(cells_f * scaled, axis=(0, 1))
    weighted = cells_f * gain_row
    grad_norm = inverse * (weighted - scaled * jnp.mean(weighted * scaled, axis=-1, keepdims=True))
    return (gain_part, (grad_stream.astype(jnp.float32) + grad_norm).astype(jnp.bfloat16))


def line_forward(regrouped, keep_mask, weights, mixing):
    channels = regrouped.shape[2]
    lined = regrouped.reshape(-1, LINE, channels)
    masked = jnp.where(keep_mask[:, :, None], lined, jnp.zeros_like(lined))
    hidden = depthwise(masked.astype(jnp.float32), weights)
    activated = jax.nn.silu(hidden).astype(jnp.bfloat16)
    mixed = jnp.dot(
        activated.reshape(-1, channels), mixing, preferred_element_type=jnp.float32
    ).astype(jnp.bfloat16)
    return (masked, hidden, activated, mixed.reshape(regrouped.shape))


def line_backward(grad_mixed, masked, hidden, activated, keep_mask, weights, mixing):
    channels = grad_mixed.shape[2]
    flat_grad = grad_mixed.reshape(-1, channels)
    mix_part = jnp.einsum(
        "nc,nd->cd", activated.reshape(-1, channels), flat_grad, preferred_element_type=jnp.float32
    )
    grad_act = jnp.einsum(
        "nd,cd->nc", flat_grad, mixing, preferred_element_type=jnp.float32
    ).reshape(hidden.shape)
    gate_value = jax.nn.sigmoid(hidden)
    grad_hidden = (grad_act * (gate_value * (1.0 + hidden * (1.0 - gate_value)))).astype(
        jnp.bfloat16
    )
    hidden_grad_f = grad_hidden.astype(jnp.float32)
    kernel_part = kernel_terms(hidden_grad_f, masked.astype(jnp.float32))
    grad_masked = depthwise_transpose(hidden_grad_f, weights)
    grad_normed = jnp.where(keep_mask[:, :, None], grad_masked, jnp.zeros_like(grad_masked)).astype(
        jnp.bfloat16
    )
    return (mix_part, kernel_part, grad_normed.reshape(grad_mixed.shape))


def body(fields, cotangent, norm_gain, kernel, mix_weight, line_order, line_starts):
    line_count = lax.axis_size("line")
    line_rank = lax.axis_index("line")
    batch_len = fields.shape[0]
    cell_count = fields.shape[1]
    positions = jnp.arange(LINE, dtype=jnp.int32)
    masks = [
        jnp.tile(positions[None, :] >= line_starts[direction][:, None], (batch_len, 1))
        for direction in range(3)
    ]
    grad_scale = float(lax.axis_size("dp") * batch_len * line_count * cell_count) ** (-0.5)
    collected = []

    def collect(mix_part, kernel_part, gain_part):
        collected.append((mix_part, kernel_part, gain_part))

    saved = []
    stream = fields
    for direction in range(3):
        values, inverse, scaled, normed = norm_forward(stream, norm_gain[direction])
        regrouped = into_lines(normed, line_order[direction], direction * line_rank, line_count)
        masked, hidden, activated, mixed = line_forward(
            regrouped, masks[direction], kernel[direction], mix_weight[direction]
        )
        returned = out_of_lines(mixed, line_order[direction], direction * line_rank, line_count)
        saved.append((inverse, scaled, masked, hidden, activated))
        stream = (values + returned.astype(jnp.float32)).astype(jnp.bfloat16)
    grad_stream = cotangent
    for direction in (2, 1, 0):
        inverse, scaled, masked, hidden, activated = saved[direction]
        grad_mixed = into_lines(
            grad_stream, line_order[direction], direction * line_rank, line_count
        )
        mix_part, kernel_part, grad_normed = line_backward(
            grad_mixed,
            masked,
            hidden,
            activated,
            masks[direction],
            kernel[direction],
            mix_weight[direction],
        )
        grad_cells = out_of_lines(
            grad_normed, line_order[direction], direction * line_rank, line_count
        )
        gain_part, grad_stream = norm_backward(
            grad_cells, inverse, scaled, norm_gain[direction], grad_stream
        )
        collect(mix_part, kernel_part, gain_part)
    ordered = collected[::-1]
    mix_stack = jnp.stack([entry[0] for entry in ordered])
    kernel_stack = jnp.stack([entry[1] for entry in ordered])
    gain_stack = jnp.stack([entry[2] for entry in ordered])
    mix_stack, kernel_stack, gain_stack = lax.psum(
        (mix_stack, kernel_stack, gain_stack), ("line", "dp")
    )
    return (
        stream,
        grad_stream,
        mix_stack * grad_scale,
        kernel_stack * grad_scale,
        gain_stack * grad_scale,
    )


def solution(mesh):
    in_specs = (
        P("dp", "line", None),
        P("dp", "line", None),
        P(),
        P(),
        P(),
        P(None, "line"),
        P(None, "line"),
    )
    out_specs = (P("dp", "line", None), P("dp", "line", None), P(), P(), P())
    return jax.shard_map(body, mesh=mesh, in_specs=in_specs, out_specs=out_specs, check_vma=False)
```

profile of v0, /device:TPU:1, one launch (start us, length us, event | category | flops | bytes accessed | tf_op | source)
XLA Modules:
  0.0 574.2 jit_solution(12604991823495048007)
XLA Ops:
  7.2 1.3 slice_bitcast_fusion.14
  12.4 10.1 %all-to-all-start = ((bf16[8,2,4096]{2,1,0:T(2,128)(2,1)}), bf16[8,2,4096]{2,1,0:T(2,128)(2,1)S(1)}, u32[]{:S(2)}, u32[]{:S(2)}) async-start(bf16[8,2,4096]{2,1,0:T(2,128)(2,1)} %reshape.868), calls=%async_computation | async-start | bytes 262144 | tf_op jit(solution)/shard_map/all_to_all | solution.py:56
  24.6 6.0 %all-to-all-done = bf16[8,2,4096]{2,1,0:T(2,128)(2,1)S(1)} async-done(((bf16[8,2,4096]{2,1,0:T(2,128)(2,1)}), bf16[8,2,4096]{2,1,0:T(2,128)(2,1)S(1)}, u32[]{:S(2)}, u32[]{:S(2)}) %all-to-all-start) | async-done | bytes 131104 | tf_op jit(solution)/shard_map/all_to_all | solution.py:56
  30.7 1.3 gather_fusion
  34.9 1.8 scatter_custom_fusion
  38.9 4.8 all-to-all-start.1
  44.9 6.9 %all-to-all-done.1 = bf16[8,2,4096]{2,1,0:T(2,128)(2,1)S(1)} async-done(((bf16[8,2,4096]{2,1,0:T(2,128)(2,1)}), bf16[8,2,4096]{2,1,0:T(2,128)(2,1)S(1)}, u32[]{:S(2)}, u32[]{:S(2)}) %all-to-all-start.1) | async-done | bytes 131104 | tf_op jit(solution)/shard_map/all_to_all | solution.py:62
  54.5 4.8 all-to-all-start.2
  60.0 7.4 %all-to-all-done.2 = bf16[8,2,4096]{2,1,0:T(2,128)(2,1)S(1)} async-done(((bf16[8,2,4096]{2,1,0:T(2,128)(2,1)}), bf16[8,2,4096]{2,1,0:T(2,128)(2,1)S(1)}, u32[]{:S(2)}, u32[]{:S(2)}) %all-to-all-start.2) | async-done | bytes 131104 | tf_op jit(solution)/shard_map/all_to_all | solution.py:56
  67.6 1.3 gather_fusion.1
  70.6 1.9 multiply_convert_fusion.1
  72.6 2.4 scatter_custom_fusion.1
  75.2 1.3 reduce.9
  77.2 4.9 all-to-all-start.3
  84.4 5.8 %all-to-all-done.3 = bf16[8,2,4096]{2,1,0:T(2,128)(2,1)S(1)} async-done(((bf16[8,2,4096]{2,1,0:T(2,128)(2,1)}), bf16[8,2,4096]{2,1,0:T(2,128)(2,1)S(1)}, u32[]{:S(2)}, u32[]{:S(2)}) %all-to-all-start.3) | async-done | bytes 131104 | tf_op jit(solution)/shard_map/all_to_all | solution.py:62
  90.2 4.8 all-to-all-start.6
  98.5 4.6 all-to-all-done.6
  103.1 5.4 all-to-all-start.4
  108.6 1.3 gather_fusion.3
  110.0 6.8 %all-to-all-done.4 = bf16[8,2,4096]{2,1,0:T(2,128)(2,1)} async-done(((bf16[8,2,4096]{2,1,0:T(2,128)(2,1)}), bf16[8,2,4096]{2,1,0:T(2,128)(2,1)}, u32[]{:S(2)}, u32[]{:S(2)}) %all-to-all-start.4) | async-done | bytes 131104 | tf_op jit(solution)/shard_map/all_to_all | solution.py:56
  116.8 1.4 reshape.877
  118.2 1.3 gather_fusion.2
  130.7 2.7 scatter_custom_fusion.2
  133.3 1.8 copy.76
  135.1 2.9 reduce.13
  138.0 1.6 reshape.878
  139.6 5.3 all-to-all-start.5
  145.5 2.9 select_convert_fusion.2
  148.5 2.3 scatter_custom_fusion.3
  153.2 7.0 %all-to-all-start.7 = ((bf16[8,2,4096]{2,1,0:T(2,128)(2,1)}), bf16[8,2,4096]{2,1,0:T(2,128)(2,1)S(1)}, u32[]{:S(2)}, u32[]{:S(2)}) async-start(bf16[8,2,4096]{2,1,0:T(2,128)(2,1)} %reshape.882), calls=%async_computation.7 | async-start | bytes 262144 | tf_op jit(solution)/shard_map/all_to_all | solution.py:62
  160.2 1.4 reshape.879
  162.3 6.0 %all-to-all-done.7 = bf16[8,2,4096]{2,1,0:T(2,128)(2,1)S(1)} async-done(((bf16[8,2,4096]{2,1,0:T(2,128)(2,1)}), bf16[8,2,4096]{2,1,0:T(2,128)(2,1)S(1)}, u32[]{:S(2)}, u32[]{:S(2)}) %all-to-all-start.7) | async-done | bytes 131104 | tf_op jit(solution)/shard_map/all_to_all | solution.py:62
  173.3 12.0 %all_to_all.60 = bf16[8,2,4096]{2,1,0:T(2,128)(2,1)S(1)} all-to-all(bf16[8,2,4096]{2,1,0:T(2,128)(2,1)S(1)} %reshape.884), channel_id=1, replica_groups=mesh['line'=8,'dp'=32] {'line'}, dimensions={0} | all-to-all | bytes 262144 | tf_op jit(solution)/shard_map/all_to_all | solution.py:56
  186.1 1.9 gather_fusion.4
  189.8 2.9 fusion.54
  194.8 1.9 scatter_custom_fusion.4
  199.0 4.8 all-to-all-start.9
  204.5 7.3 %all-to-all-done.9 = bf16[8,2,4096]{2,1,0:T(2,128)(2,1)S(1)} async-done(((bf16[8,2,4096]{2,1,0:T(2,128)(2,1)}), bf16[8,2,4096]{2,1,0:T(2,128)(2,1)S(1)}, u32[]{:S(2)}, u32[]{:S(2)}) %all-to-all-start.9) | async-done | bytes 131104 | tf_op jit(solution)/shard_map/all_to_all | solution.py:62
  215.8 4.9 all-to-all-start.10
  223.5 5.3 all-to-all-done.10
  229.6 1.3 gather_fusion.5
  232.1 2.2 fusion.52
  237.4 1.9 select_convert_fusion
  239.3 2.1 scatter_custom_fusion.5
  243.8 4.8 all-to-all-start.11
  249.3 236.4 %all-reduce.87.cloned.1.call-done = f32[3,128,128]{2,1,0:T(8,128)} async-done(((f32[3,128,128]{2,1,0:T(8,128)}), f32[3,128,128]{2,1,0:T(8,128)}) %all-reduce.87.cloned.1.call-update) | async-done | bytes 196624 | tf_op jit(solution)/shard_map/psum | solution.py:169
  485.8 1.6 broadcast_multiply_fusion
  489.0 76.0 %all-reduce.84 = (f32[3,15,128]{2,1,0:T(8,128)S(1)}, f32[3,128]{1,0:T(4,128)S(1)}) all-reduce(f32[3,15,128]{2,1,0:T(8,128)S(1)} %pad_maximum_fusion.1, f32[3,128]{1,0:T(4,128)S(1)} %pad_maximum_fusion.2), channel_id=1, replica_groups=mesh['line'=8,'dp'=32] {'line','dp'}, use_global_device_ids=true, to_apply=%region_58.62 | all-reduce | flops 6144 | bytes 49152 | tf_op jit(solution)/shard_map/psum | solution.py:169
  (491 shorter events, 68.5 us)
Async XLA Ops:
  8.5 43.6 %copy-start.48 = (f32[128]{0:T(128)}, f32[128]{0:T(128)S(1)}, u32[]{:S(2)}) copy-start(f32[128]{0:T(128)S(1)} %get-tuple-element.213) | copy-start | bytes 1540
  12.4 10.1 %copy-start.43 = (s32[3,512]{1,0:T(4,128)S(1)}, s32[3,512]{1,0:T(4,128)}, u32[]{:S(2)}) copy-start(s32[3,512]{1,0:T(4,128)} %param.18) | copy-start | bytes 18436
  12.4 10.1 %copy-start.42 = (f32[3,15,128]{2,1,0:T(8,128)S(1)}, f32[3,15,128]{2,1,0:T(8,128)}, u32[]{:S(2)}) copy-start(f32[3,15,128]{2,1,0:T(8,128)} %param.16) | copy-start | bytes 69124
  12.4 18.1 %all-to-all-start = ((bf16[8,2,4096]{2,1,0:T(2,128)(2,1)}), bf16[8,2,4096]{2,1,0:T(2,128)(2,1)S(1)}, u32[]{:S(2)}, u32[]{:S(2)}) async-start(bf16[8,2,4096]{2,1,0:T(2,128)(2,1)} %reshape.868), calls=%async_computation | async-start | bytes 262144 | tf_op jit(solution)/shard_map/all_to_all | solution.py:56
  22.5 9.5 %copy-start.82 = (pred[512]{0:T(512)(128)(4,1)}, pred[512]{0:T(512)(128)(4,1)S(1)}, u32[]{:S(2)}) copy-start(pred[512]{0:T(512)(128)(4,1)S(1)} %compare_and_fusion.2) | copy-start | bytes 1540
  23.1 9.6 %copy-start.59 = (f32[128]{0:T(128)}, f32[128]{0:T(128)S(1)}, u32[]{:S(2)}) copy-start(f32[128]{0:T(128)S(1)} %get-tuple-element.196) | copy-start | bytes 1540
  23.1 9.6 %copy-start.61 = (f32[128]{0:T(128)}, f32[128]{0:T(128)S(1)}, u32[]{:S(2)}) copy-start(f32[128]{0:T(128)S(1)} %get-tuple-element.197) | copy-start | bytes 1540
  23.1 9.6 %copy-start.63 = (f32[128]{0:T(128)}, f32[128]{0:T(128)S(1)}, u32[]{:S(2)}) copy-start(f32[128]{0:T(128)S(1)} %get-tuple-element.198) | copy-start | bytes 1540
  23.1 9.6 %copy-start.65 = (f32[128]{0:T(128)}, f32[128]{0:T(128)S(1)}, u32[]{:S(2)}) copy-start(f32[128]{0:T(128)S(1)} %get-tuple-element.199) | copy-start | bytes 1540
  23.1 9.7 %copy-start.67 = (f32[128]{0:T(128)}, f32[128]{0:T(128)S(1)}, u32[]{:S(2)}) copy-start(f32[128]{0:T(128)S(1)} %get-tuple-element.200) | copy-start | bytes 1540
  23.1 9.7 %copy-start.69 = (f32[128]{0:T(128)}, f32[128]{0:T(128)S(1)}, u32[]{:S(2)}) copy-start(f32[128]{0:T(128)S(1)} %get-tuple-element.201) | copy-start | bytes 1540
  23.8 9.0 %copy-start.73 = (f32[128]{0:T(128)}, f32[128]{0:T(128)S(1)}, u32[]{:S(2)}) copy-start(f32[128]{0:T(128)S(1)} %get-tuple-element.186) | copy-start | bytes 1540
  23.8 9.0 %copy-start.74 = (f32[128]{0:T(128)}, f32[128]{0:T(128)S(1)}, u32[]{:S(2)}) copy-start(f32[128]{0:T(128)S(1)} %get-tuple-element.187) | copy-start | bytes 1540
  23.8 9.0 %copy-start.75 = (f32[128]{0:T(128)}, f32[128]{0:T(128)S(1)}, u32[]{:S(2)}) copy-start(f32[128]{0:T(128)S(1)} %get-tuple-element.188) | copy-start | bytes 1540
  23.8 9.0 %copy-start.76 = (f32[128]{0:T(128)}, f32[128]{0:T(128)S(1)}, u32[]{:S(2)}) copy-start(f32[128]{0:T(128)S(1)} %get-tuple-element.189) | copy-start | bytes 1540
  23.8 9.0 %copy-start.77 = (f32[128]{0:T(128)}, f32[128]{0:T(128)S(1)}, u32[]{:S(2)}) copy-start(f32[128]{0:T(128)S(1)} %get-tuple-element.190) | copy-start | bytes 1540
  23.8 9.0 %copy-start.78 = (f32[128]{0:T(128)}, f32[128]{0:T(128)S(1)}, u32[]{:S(2)}) copy-start(f32[128]{0:T(128)S(1)} %get-tuple-element.191) | copy-start | bytes 1540
  23.8 9.0 %copy-start.79 = (f32[128]{0:T(128)}, f32[128]{0:T(128)S(1)}, u32[]{:S(2)}) copy-start(f32[128]{0:T(128)S(1)} %get-tuple-element.192) | copy-start | bytes 1540
  23.9 9.0 %copy-start.80 = (f32[128]{0:T(128)}, f32[128]{0:T(128)S(1)}, u32[]{:S(2)}) copy-start(f32[128]{0:T(128)S(1)} %get-tuple-element.193) | copy-start | bytes 1540
  23.9 9.0 %copy-start.81 = (f32[128]{0:T(128)}, f32[128]{0:T(128)S(1)}, u32[]{:S(2)}) copy-start(f32[128]{0:T(128)S(1)} %get-tuple-element.194) | copy-start | bytes 1540
  24.0 8.9 %copy-start.57 = (pred[4,128]{1,0:T(4,128)(4,1)}, pred[4,128]{1,0:T(4,128)(4,1)S(1)}, u32[]{:S(2)}) copy-start(pred[4,128]{1,0:T(4,128)(4,1)S(1)} %iota_compare_fusion.2) | copy-start | bytes 1540
  24.0 6.7 %copy-start.44 = (s32[1024]{0:T(1024)}, s32[1024]{0:T(1024)S(1)}, u32[]{:S(2)}) copy-start(s32[1024]{0:T(1024)S(1)} %pad_clamp_fusion.2) | copy-start | bytes 12292
  24.6 10.4 %copy-start.117 = (s32[512,1]{0,1:T(1,128)}, s32[512,1]{0,1:T(1,128)S(1)}, u32[]{:S(2)}) copy-start(s32[512,1]{0,1:T(1,128)S(1)} %get-tuple-element.206) | copy-start | bytes 6148
  38.9 12.9 %all-to-all-start.1 = ((bf16[8,2,4096]{2,1,0:T(2,128)(2,1)}), bf16[8,2,4096]{2,1,0:T(2,128)(2,1)S(1)}, u32[]{:S(2)}, u32[]{:S(2)}) async-start(bf16[8,2,4096]{2,1,0:T(2,128)(2,1)} %reshape.870), calls=%async_computation.1 | async-start | bytes 262144 | tf_op jit(solution)/shard_map/all_to_all | solution.py:62
  44.3 25.3 %copy-start.50 = (pred[4,128]{1,0:T(4,128)(4,1)}, pred[4,128]{1,0:T(4,128)(4,1)S(1)}, u32[]{:S(2)}) copy-start(pred[4,128]{1,0:T(4,128)(4,1)S(1)} %get-tuple-element.222) | copy-start | bytes 1540
  44.9 24.1 %copy-start.98 = (pred[512]{0:T(512)(128)(4,1)}, pred[512]{0:T(512)(128)(4,1)S(1)}, u32[]{:S(2)}) copy-start(pred[512]{0:T(512)(128)(4,1)S(1)} %get-tuple-element.220) | copy-start | bytes 1540
  54.5 12.9 %all-to-all-start.2 = ((bf16[8,2,4096]{2,1,0:T(2,128)(2,1)}), bf16[8,2,4096]{2,1,0:T(2,128)(2,1)S(1)}, u32[]{:S(2)}, u32[]{:S(2)}) async-start(bf16[8,2,4096]{2,1,0:T(2,128)(2,1)} %reshape.872), calls=%async_computation.2 | async-start | bytes 262144 | tf_op jit(solution)/shard_map/all_to_all | solution.py:56
  59.4 8.2 %copy-start.46 = (s32[1024]{0:T(1024)}, s32[1024]{0:T(1024)S(1)}, u32[]{:S(2)}) copy-start(s32[1024]{0:T(1024)S(1)} %pad_clamp_fusion.1) | copy-start | bytes 12292
  60.0 9.6 %copy-start.84 = (f32[128]{0:T(128)}, f32[128]{0:T(128)S(1)}, u32[]{:S(2)}) copy-start(f32[128]{0:T(128)S(1)} %get-tuple-element.170) | copy-start | bytes 1540
  60.0 9.6 %copy-start.86 = (f32[128]{0:T(128)}, f32[128]{0:T(128)S(1)}, u32[]{:S(2)}) copy-start(f32[128]{0:T(128)S(1)} %get-tuple-element.171) | copy-start | bytes 1540
  60.0 9.6 %copy-start.88 = (f32[128]{0:T(128)}, f32[128]{0:T(128)S(1)}, u32[]{:S(2)}) copy-start(f32[128]{0:T(128)S(1)} %get-tuple-element.172) | copy-start | bytes 1540
  60.0 9.6 %copy-start.90 = (f32[128]{0:T(128)}, f32[128]{0:T(128)S(1)}, u32[]{:S(2)}) copy-start(f32[128]{0:T(128)S(1)} %get-tuple-element.173) | copy-start | bytes 1540
  60.0 9.6 %copy-start.92 = (f32[128]{0:T(128)}, f32[128]{0:T(128)S(1)}, u32[]{:S(2)}) copy-start(f32[128]{0:T(128)S(1)} %get-tuple-element.174) | copy-start | bytes 1540
  60.0 9.6 %copy-start.94 = (f32[128]{0:T(128)}, f32[128]{0:T(128)S(1)}, u32[]{:S(2)}) copy-start(f32[128]{0:T(128)S(1)} %get-tuple-element.175) | copy-start | bytes 1540
  77.2 13.0 %all-to-all-start.3 = ((bf16[8,2,4096]{2,1,0:T(2,128)(2,1)}), bf16[8,2,4096]{2,1,0:T(2,128)(2,1)S(1)}, u32[]{:S(2)}, u32[]{:S(2)}) async-start(bf16[8,2,4096]{2,1,0:T(2,128)(2,1)} %reshape.874), calls=%async_computation.3 | async-start | bytes 262144 | tf_op jit(solution)/shard_map/all_to_all | solution.py:62
  90.2 12.9 %all-to-all-start.6 = ((bf16[8,2,4096]{2,1,0:T(2,128)(2,1)}), bf16[8,2,4096]{2,1,0:T(2,128)(2,1)S(1)}, u32[]{:S(2)}, u32[]{:S(2)}) async-start(bf16[8,2,4096]{2,1,0:T(2,128)(2,1)} %reshape.880), calls=%async_computation.6 | async-start | bytes 262144 | tf_op jit(solution)/shard_map/all_to_all | solution.py:56
  103.1 13.7 %all-to-all-start.4 = ((bf16[8,2,4096]{2,1,0:T(2,128)(2,1)}), bf16[8,2,4096]{2,1,0:T(2,128)(2,1)}, u32[]{:S(2)}, u32[]{:S(2)}) async-start(bf16[8,2,4096]{2,1,0:T(2,128)(2,1)} %reshape.876), calls=%async_computation.4 | async-start | bytes 262144 | tf_op jit(solution)/shard_map/all_to_all | solution.py:56
  139.6 13.6 %all-to-all-start.5 = ((bf16[8,2,4096]{2,1,0:T(2,128)(2,1)}), bf16[8,2,4096]{2,1,0:T(2,128)(2,1)}, u32[]{:S(2)}, u32[]{:S(2)}) async-start(bf16[8,2,4096]{2,1,0:T(2,128)(2,1)} %reshape.878), calls=%async_computation.5 | async-start | bytes 262144 | tf_op jit(solution)/shard_map/all_to_all | solution.py:62
  153.2 15.1 %all-to-all-start.7 = ((bf16[8,2,4096]{2,1,0:T(2,128)(2,1)}), bf16[8,2,4096]{2,1,0:T(2,128)(2,1)S(1)}, u32[]{:S(2)}, u32[]{:S(2)}) async-start(bf16[8,2,4096]{2,1,0:T(2,128)(2,1)} %reshape.882), calls=%async_computation.7 | async-start | bytes 262144 | tf_op jit(solution)/shard_map/all_to_all | solution.py:62
  198.2 5.6 copy-start.122
  198.2 5.6 copy-start.123
  198.2 5.6 copy-start.124
  198.2 5.6 copy-start.125
  198.2 5.6 copy-start.126
  199.0 12.9 %all-to-all-start.9 = ((bf16[8,2,4096]{2,1,0:T(2,128)(2,1)}), bf16[8,2,4096]{2,1,0:T(2,128)(2,1)S(1)}, u32[]{:S(2)}, u32[]{:S(2)}) async-start(bf16[8,2,4096]{2,1,0:T(2,128)(2,1)} %reshape.886), calls=%async_computation.9 | async-start | bytes 262144 | tf_op jit(solution)/shard_map/all_to_all | solution.py:62
  215.8 13.0 %all-to-all-start.10 = ((bf16[8,2,4096]{2,1,0:T(2,128)(2,1)}), bf16[8,2,4096]{2,1,0:T(2,128)(2,1)S(1)}, u32[]{:S(2)}, u32[]{:S(2)}) async-start(bf16[8,2,4096]{2,1,0:T(2,128)(2,1)} %reshape.888), calls=%async_computation.10 | async-start | bytes 262144 | tf_op jit(solution)/shard_map/all_to_all | solution.py:56
  220.7 265.0 %all-reduce.87.cloned.1.call-start = ((), (), s32[]{:S(2)}) async-start(), calls=%async_computation.12 | async-start | bytes 393216 | tf_op jit(solution)/shard_map/psum | solution.py:169
  243.8 243.6 %all-to-all-start.11 = ((bf16[8,2,4096]{2,1,0:T(2,128)(2,1)}), bf16[8,2,4096]{2,1,0:T(2,128)(2,1)S(1)}, u32[]{:S(2)}, u32[]{:S(2)}) async-start(bf16[8,2,4096]{2,1,0:T(2,128)(2,1)} %reshape.890), calls=%async_computation.11 | async-start | bytes 262144 | tf_op jit(solution)/shard_map/all_to_all | solution.py:62
  (126 other events, 213.1 us)
Sparse Core Ops, SparseCore 0:
  236.8 248.8 all-reduce.86
where the time goes:
time: 584 us; the launch traced here: 574 us
  waiting for transfers between devices  293 us (50%)
  blocking collectives  88 us (15%)
  local copies, waits for them, and re-layouts  65.5 us (11%)
  starting transfers between devices  61.9 us (11%)
  other arithmetic  39.9 us (7%)
  between operations  16.8 us (3%)
  matrix products  9.42 us (2%)
    psum x1, waiting for transfers between devices, body(): lax.psum((mix_stack, kernel_stack, gain_stack), ('line', 'dp'))  236 us
    psum x1, blocking collectives, body(): lax.psum((mix_stack, kernel_stack, gain_stack), ('line', 'dp'))  76 us
    all_to_all x6, starting transfers between devices, out_of_lines(): lax.all_to_all(placed, 'line', split_axis=1, concat_axis=1, tiled=True)  31.7 us
    all_to_all x5, starting transfers between devices, into_lines(): lax.all_to_all(rolled, 'line', split_axis=1, concat_axis=1, tiled=True)  30 us
    all_to_all x5, waiting for transfers between devices, into_lines(): lax.all_to_all(rolled, 'line', split_axis=1, concat_axis=1, tiled=True)  30 us
    unnamed x359, local copies, waits for them, and re-layouts  29.1 us
    all_to_all x6, waiting for transfers between devices, out_of_lines(): lax.all_to_all(placed, 'line', split_axis=1, concat_axis=1, tiled=True)  26.2 us
    unnamed x12, other arithmetic  17.3 us
  transfers between devices with their start and end apart: 12, of which 11 were waited for; matrix products, arithmetic and copies ran while one was open for 5% of the time, Pallas kernels for 0%

commit v1 on v0

--- a/solution.py
+++ b/solution.py
@@ -59,7 +59,10 @@
 
 def out_of_lines(array, table, shift, line_count):
     placed = unpermute(array, table)
-    received = lax.all_to_all(placed, "line", split_axis=1, concat_axis=1, tiled=True)
+    received = jnp.concatenate(
+        lax.all_to_all(jnp.stack(jnp.split(placed, lax.axis_size("line"), axis=1)), "line", 0, 0),
+        axis=1,
+    )
     return jnp.roll(block_view(received, line_count), -shift, axis=1).reshape(array.shape)
 
 

time: 584 us -> 585 us (level); the launches traced: 574 us -> 583 us
  local copies, waits for them, and re-layouts: 65.5 us -> 84.3 us
  other arithmetic: 39.9 us -> 32.4 us
    unnamed x359 -> x381, local copies, waits for them, and re-layouts: 29.1 us -> 47.9 us
    unnamed x12 -> x6, other arithmetic: 17.3 us -> 8.22 us
    scatter x12 -> x6, local copies, waits for them, and re-layouts: 16 us -> 12.5 us  [unpermute(): return jnp.zeros_like(array).at[:, table].set(array)]
  transfers between devices with their start and end apart: 12 -> 12, of which waited for: 11 -> 10; matrix products, arithmetic and copies ran while one was open for 5% -> 6% of each run, Pallas kernels for 0% -> 0%
where the time goes in v1:
time: 585 us; the launch traced here: 583 us
  waiting for transfers between devices  291 us (50%)
  blocking collectives  88.2 us (15%)
  local copies, waits for them, and re-layouts  84.3 us (14%)
  starting transfers between devices  61.1 us (10%)
  other arithmetic  32.4 us (6%)
  between operations  16.4 us (3%)
  matrix products  9.42 us (2%)
    psum x1, waiting for transfers between devices, body(): lax.psum((mix_stack, kernel_stack, gain_stack), ('line', 'dp'))  234 us
    psum x1, blocking collectives, body(): lax.psum((mix_stack, kernel_stack, gain_stack), ('line', 'dp'))  76 us
    unnamed x381, local copies, waits for them, and re-layouts  47.9 us
    all_to_all x6, starting transfers between devices, out_of_lines(): lax.all_to_all(jnp.stack(jnp.split(placed, lax.axis_size('line'), axis=1)...  31.4 us
    all_to_all x5, waiting for transfers between devices, into_lines(): lax.all_to_all(rolled, 'line', split_axis=1, concat_axis=1, tiled=True)  30.4 us
    all_to_all x5, starting transfers between devices, into_lines(): lax.all_to_all(rolled, 'line', split_axis=1, concat_axis=1, tiled=True)  29.7 us
    all_to_all x6, waiting for transfers between devices, out_of_lines(): lax.all_to_all(jnp.stack(jnp.split(placed, lax.axis_size('line'), axis=1)...  27.4 us
    scatter x6, local copies, waits for them, and re-layouts, unpermute(): return jnp.zeros_like(array).at[:, table].set(array)  12.5 us
  transfers between devices with their start and end apart: 12, of which 10 were waited for; matrix products, arithmetic and copies ran while one was open for 6% of the time, Pallas kernels for 0%

profile of v1, /device:TPU:1, one launch (start us, length us, event | category | flops | bytes accessed | tf_op | source)
XLA Modules:
  0.0 583.1 jit_solution(1416312670809422318)
XLA Ops:
  10.0 1.4 reduce.6
  12.0 10.1 %all-to-all-start = ((bf16[8,2,4096]{2,1,0:T(2,128)(2,1)}), bf16[8,2,4096]{2,1,0:T(2,128)(2,1)S(1)}, u32[]{:S(2)}, u32[]{:S(2)}) async-start(bf16[8,2,4096]{2,1,0:T(2,128)(2,1)} %reshape.868), calls=%async_computation | async-start | bytes 262144 | tf_op jit(solution)/shard_map/all_to_all | solution.py:56
  24.3 5.9 %all-to-all-done = bf16[8,2,4096]{2,1,0:T(2,128)(2,1)S(1)} async-done(((bf16[8,2,4096]{2,1,0:T(2,128)(2,1)}), bf16[8,2,4096]{2,1,0:T(2,128)(2,1)S(1)}, u32[]{:S(2)}, u32[]{:S(2)}) %all-to-all-start) | async-done | bytes 131104 | tf_op jit(solution)/shard_map/all_to_all | solution.py:56
  30.3 1.3 gather_fusion
  34.5 1.8 scatter_custom_fusion
  41.2 4.8 all-to-all-start.1
  47.1 7.0 %all-to-all-done.1 = bf16[8,1,64,128]{3,2,1,0:T(8,128)(2,1)S(1)} async-done(((bf16[8,1,64,128]{3,2,1,0:T(8,128)(2,1)}), bf16[8,1,64,128]{3,2,1,0:T(8,128)(2,1)S(1)}, u32[]{:S(2)}, u32[]{:S(2)}) %all-to-all-start.1) | async-done | bytes 131104 | tf_op jit(solution)/shard_map/all_to_all | solution.py:63
  54.7 1.4 reduce.7
  56.8 4.7 all-to-all-start.2
  62.8 6.9 %all-to-all-done.2 = bf16[8,2,4096]{2,1,0:T(2,128)(2,1)S(1)} async-done(((bf16[8,2,4096]{2,1,0:T(2,128)(2,1)}), bf16[8,2,4096]{2,1,0:T(2,128)(2,1)S(1)}, u32[]{:S(2)}, u32[]{:S(2)}) %all-to-all-start.2) | async-done | bytes 131104 | tf_op jit(solution)/shard_map/all_to_all | solution.py:56
  69.8 1.3 gather_fusion.1
  72.8 1.8 multiply_convert_fusion.1
  74.8 1.9 scatter_custom_fusion.1
  81.6 4.8 all-to-all-start.3
  86.7 1.4 reduce.8
  88.8 5.8 %all-to-all-done.3 = bf16[8,1,64,128]{3,2,1,0:T(8,128)(2,1)S(1)} async-done(((bf16[8,1,64,128]{3,2,1,0:T(8,128)(2,1)}), bf16[8,1,64,128]{3,2,1,0:T(8,128)(2,1)S(1)}, u32[]{:S(2)}, u32[]{:S(2)}) %all-to-all-start.3) | async-done | bytes 131104 | tf_op jit(solution)/shard_map/all_to_all | solution.py:63
  94.6 4.7 all-to-all-start.6
  100.0 1.4 reduce.9
  102.0 5.3 all-to-all-done.6
  107.3 5.4 all-to-all-start.4
  112.9 1.5 gather_fusion.3
  114.4 6.7 %all-to-all-done.4 = bf16[8,2,4096]{2,1,0:T(2,128)(2,1)} async-done(((bf16[8,2,4096]{2,1,0:T(2,128)(2,1)}), bf16[8,2,4096]{2,1,0:T(2,128)(2,1)}, u32[]{:S(2)}, u32[]{:S(2)}) %all-to-all-start.4) | async-done | bytes 131104 | tf_op jit(solution)/shard_map/all_to_all | solution.py:56
  121.0 1.4 reshape.873
  122.4 1.5 gather_fusion.2
  135.1 2.7 scatter_custom_fusion.2
  137.8 1.4 constant_dynamic-update-slice_fusion.23
  145.6 5.3 all-to-all-start.5
  151.5 2.9 select_convert_fusion.2
  154.4 2.1 scatter_custom_fusion.3
  161.4 7.2 %all-to-all-start.7 = ((bf16[8,1,64,128]{3,2,1,0:T(8,128)(2,1)}), bf16[8,1,64,128]{3,2,1,0:T(8,128)(2,1)S(1)}, u32[]{:S(2)}, u32[]{:S(2)}) async-start(bf16[8,1,64,128]{3,2,1,0:T(8,128)(2,1)} %constant_dynamic-update-slice_fusion.24), calls=%async_computation.7 | async-start | bytes 262144 | tf_op jit(solution)/shard_map/all_to_all | solution.py:63
  169.6 7.1 %all-to-all-done.7 = bf16[8,1,64,128]{3,2,1,0:T(8,128)(2,1)S(1)} async-done(((bf16[8,1,64,128]{3,2,1,0:T(8,128)(2,1)}), bf16[8,1,64,128]{3,2,1,0:T(8,128)(2,1)S(1)}, u32[]{:S(2)}, u32[]{:S(2)}) %all-to-all-start.7) | async-done | bytes 131104 | tf_op jit(solution)/shard_map/all_to_all | solution.py:63
  179.3 1.4 reduce.10
  180.7 12.2 %all_to_all.60 = bf16[8,2,4096]{2,1,0:T(2,128)(2,1)S(1)} all-to-all(bf16[8,2,4096]{2,1,0:T(2,128)(2,1)S(1)} %reshape.876), channel_id=1, replica_groups=mesh['line'=8,'dp'=32] {'line'}, dimensions={0} | all-to-all | bytes 262144 | tf_op jit(solution)/shard_map/all_to_all | solution.py:56
  193.1 1.9 gather_fusion.4
  196.7 2.9 fusion.54
  201.8 1.9 scatter_custom_fusion.4
  208.6 4.6 all-to-all-start.9
  213.9 7.4 %all-to-all-done.9 = bf16[8,1,64,128]{3,2,1,0:T(8,128)(2,1)S(1)} async-done(((bf16[8,1,64,128]{3,2,1,0:T(8,128)(2,1)}), bf16[8,1,64,128]{3,2,1,0:T(8,128)(2,1)S(1)}, u32[]{:S(2)}, u32[]{:S(2)}) %all-to-all-start.9) | async-done | bytes 131104 | tf_op jit(solution)/shard_map/all_to_all | solution.py:63
  223.2 1.4 reduce.11
  225.2 4.8 all-to-all-start.10
  232.6 5.6 all-to-all-done.10
  241.5 2.2 fusion.52
  246.9 1.9 select_convert_fusion
  248.8 2.1 scatter_custom_fusion.5
  255.9 4.7 all-to-all-start.11
  261.3 233.6 %all-reduce.87.cloned.1.call-done = f32[3,128,128]{2,1,0:T(8,128)} async-done(((f32[3,128,128]{2,1,0:T(8,128)}), f32[3,128,128]{2,1,0:T(8,128)}) %all-reduce.87.cloned.1.call-update) | async-done | bytes 196624 | tf_op jit(solution)/shard_map/psum | solution.py:172
  495.0 1.6 broadcast_multiply_fusion
  498.2 76.0 %all-reduce.84 = (f32[3,15,128]{2,1,0:T(8,128)S(1)}, f32[3,128]{1,0:T(4,128)S(1)}) all-reduce(f32[3,15,128]{2,1,0:T(8,128)S(1)} %pad_maximum_fusion.1, f32[3,128]{1,0:T(4,128)S(1)} %pad_maximum_fusion.2), channel_id=1, replica_groups=mesh['line'=8,'dp'=32] {'line','dp'}, use_global_device_ids=true, to_apply=%region_58.62 | all-reduce | flops 6144 | bytes 49152 | tf_op jit(solution)/shard_map/psum | solution.py:172
  (506 shorter events, 81.6 us)
Async XLA Ops:
  8.0 46.3 %copy-start.48 = (f32[128]{0:T(128)}, f32[128]{0:T(128)S(1)}, u32[]{:S(2)}) copy-start(f32[128]{0:T(128)S(1)} %get-tuple-element.213) | copy-start | bytes 1540
  8.0 91.5 %copy-start.54 = (f32[128]{0:T(128)}, f32[128]{0:T(128)S(1)}, u32[]{:S(2)}) copy-start(f32[128]{0:T(128)S(1)} %get-tuple-element.211) | copy-start | bytes 1540
  12.0 10.1 %copy-start.43 = (s32[3,512]{1,0:T(4,128)S(1)}, s32[3,512]{1,0:T(4,128)}, u32[]{:S(2)}) copy-start(s32[3,512]{1,0:T(4,128)} %param.18) | copy-start | bytes 18436
  12.0 10.1 %copy-start.42 = (f32[3,15,128]{2,1,0:T(8,128)S(1)}, f32[3,15,128]{2,1,0:T(8,128)}, u32[]{:S(2)}) copy-start(f32[3,15,128]{2,1,0:T(8,128)} %param.16) | copy-start | bytes 69124
  12.0 18.1 %all-to-all-start = ((bf16[8,2,4096]{2,1,0:T(2,128)(2,1)}), bf16[8,2,4096]{2,1,0:T(2,128)(2,1)S(1)}, u32[]{:S(2)}, u32[]{:S(2)}) async-start(bf16[8,2,4096]{2,1,0:T(2,128)(2,1)} %reshape.868), calls=%async_computation | async-start | bytes 262144 | tf_op jit(solution)/shard_map/all_to_all | solution.py:56
  22.1 9.5 %copy-start.81 = (pred[512]{0:T(512)(128)(4,1)}, pred[512]{0:T(512)(128)(4,1)S(1)}, u32[]{:S(2)}) copy-start(pred[512]{0:T(512)(128)(4,1)S(1)} %compare_and_fusion.2) | copy-start | bytes 1540
  22.8 9.6 %copy-start.58 = (f32[128]{0:T(128)}, f32[128]{0:T(128)S(1)}, u32[]{:S(2)}) copy-start(f32[128]{0:T(128)S(1)} %get-tuple-element.196) | copy-start | bytes 1540
  22.8 9.6 %copy-start.60 = (f32[128]{0:T(128)}, f32[128]{0:T(128)S(1)}, u32[]{:S(2)}) copy-start(f32[128]{0:T(128)S(1)} %get-tuple-element.197) | copy-start | bytes 1540
  22.8 9.6 %copy-start.62 = (f32[128]{0:T(128)}, f32[128]{0:T(128)S(1)}, u32[]{:S(2)}) copy-start(f32[128]{0:T(128)S(1)} %get-tuple-element.198) | copy-start | bytes 1540
  22.8 9.6 %copy-start.64 = (f32[128]{0:T(128)}, f32[128]{0:T(128)S(1)}, u32[]{:S(2)}) copy-start(f32[128]{0:T(128)S(1)} %get-tuple-element.199) | copy-start | bytes 1540
  22.8 9.6 %copy-start.66 = (f32[128]{0:T(128)}, f32[128]{0:T(128)S(1)}, u32[]{:S(2)}) copy-start(f32[128]{0:T(128)S(1)} %get-tuple-element.200) | copy-start | bytes 1540
  22.8 9.6 %copy-start.68 = (f32[128]{0:T(128)}, f32[128]{0:T(128)S(1)}, u32[]{:S(2)}) copy-start(f32[128]{0:T(128)S(1)} %get-tuple-element.201) | copy-start | bytes 1540
  23.5 8.9 %copy-start.72 = (f32[128]{0:T(128)}, f32[128]{0:T(128)S(1)}, u32[]{:S(2)}) copy-start(f32[128]{0:T(128)S(1)} %get-tuple-element.186) | copy-start | bytes 1540
  23.5 8.9 %copy-start.73 = (f32[128]{0:T(128)}, f32[128]{0:T(128)S(1)}, u32[]{:S(2)}) copy-start(f32[128]{0:T(128)S(1)} %get-tuple-element.187) | copy-start | bytes 1540
  23.5 8.9 %copy-start.74 = (f32[128]{0:T(128)}, f32[128]{0:T(128)S(1)}, u32[]{:S(2)}) copy-start(f32[128]{0:T(128)S(1)} %get-tuple-element.188) | copy-start | bytes 1540
  23.5 8.9 %copy-start.75 = (f32[128]{0:T(128)}, f32[128]{0:T(128)S(1)}, u32[]{:S(2)}) copy-start(f32[128]{0:T(128)S(1)} %get-tuple-element.189) | copy-start | bytes 1540
  23.5 8.9 %copy-start.76 = (f32[128]{0:T(128)}, f32[128]{0:T(128)S(1)}, u32[]{:S(2)}) copy-start(f32[128]{0:T(128)S(1)} %get-tuple-element.190) | copy-start | bytes 1540
  23.5 8.9 %copy-start.77 = (f32[128]{0:T(128)}, f32[128]{0:T(128)S(1)}, u32[]{:S(2)}) copy-start(f32[128]{0:T(128)S(1)} %get-tuple-element.191) | copy-start | bytes 1540
  23.5 8.9 %copy-start.78 = (f32[128]{0:T(128)}, f32[128]{0:T(128)S(1)}, u32[]{:S(2)}) copy-start(f32[128]{0:T(128)S(1)} %get-tuple-element.192) | copy-start | bytes 1540
  23.5 8.9 %copy-start.79 = (f32[128]{0:T(128)}, f32[128]{0:T(128)S(1)}, u32[]{:S(2)}) copy-start(f32[128]{0:T(128)S(1)} %get-tuple-element.193) | copy-start | bytes 1540
  23.5 8.9 %copy-start.80 = (f32[128]{0:T(128)}, f32[128]{0:T(128)S(1)}, u32[]{:S(2)}) copy-start(f32[128]{0:T(128)S(1)} %get-tuple-element.194) | copy-start | bytes 1540
  23.6 8.8 %copy-start.56 = (pred[4,128]{1,0:T(4,128)(4,1)}, pred[4,128]{1,0:T(4,128)(4,1)S(1)}, u32[]{:S(2)}) copy-start(pred[4,128]{1,0:T(4,128)(4,1)S(1)} %iota_compare_fusion.2) | copy-start | bytes 1540
  23.6 6.7 %copy-start.44 = (s32[1024]{0:T(1024)}, s32[1024]{0:T(1024)S(1)}, u32[]{:S(2)}) copy-start(s32[1024]{0:T(1024)S(1)} %pad_clamp_fusion.2) | copy-start | bytes 12292
  24.3 10.2 %copy-start.115 = (s32[512,1]{0,1:T(1,128)}, s32[512,1]{0,1:T(1,128)S(1)}, u32[]{:S(2)}) copy-start(s32[512,1]{0,1:T(1,128)S(1)} %get-tuple-element.206) | copy-start | bytes 6148
  41.2 13.0 %all-to-all-start.1 = ((bf16[8,1,64,128]{3,2,1,0:T(8,128)(2,1)}), bf16[8,1,64,128]{3,2,1,0:T(8,128)(2,1)S(1)}, u32[]{:S(2)}, u32[]{:S(2)}) async-start(bf16[8,1,64,128]{3,2,1,0:T(8,128)(2,1)} %constant_dynamic-update-slice_fusion), calls=%async_computation.1 | async-start | bytes 262144 | tf_op jit(solution)/shard_map/all_to_all | solution.py:63
  46.6 25.3 %copy-start.50 = (pred[4,128]{1,0:T(4,128)(4,1)}, pred[4,128]{1,0:T(4,128)(4,1)S(1)}, u32[]{:S(2)}) copy-start(pred[4,128]{1,0:T(4,128)(4,1)S(1)} %get-tuple-element.224) | copy-start | bytes 1540
  47.1 24.1 %copy-start.97 = (pred[512]{0:T(512)(128)(4,1)}, pred[512]{0:T(512)(128)(4,1)S(1)}, u32[]{:S(2)}) copy-start(pred[512]{0:T(512)(128)(4,1)S(1)} %get-tuple-element.220) | copy-start | bytes 1540
  56.8 12.9 %all-to-all-start.2 = ((bf16[8,2,4096]{2,1,0:T(2,128)(2,1)}), bf16[8,2,4096]{2,1,0:T(2,128)(2,1)S(1)}, u32[]{:S(2)}, u32[]{:S(2)}) async-start(bf16[8,2,4096]{2,1,0:T(2,128)(2,1)} %reshape.870), calls=%async_computation.2 | async-start | bytes 262144 | tf_op jit(solution)/shard_map/all_to_all | solution.py:56
  62.7 9.2 %copy-start.83 = (f32[128]{0:T(128)}, f32[128]{0:T(128)S(1)}, u32[]{:S(2)}) copy-start(f32[128]{0:T(128)S(1)} %get-tuple-element.170) | copy-start | bytes 1540
  62.7 9.2 %copy-start.85 = (f32[128]{0:T(128)}, f32[128]{0:T(128)S(1)}, u32[]{:S(2)}) copy-start(f32[128]{0:T(128)S(1)} %get-tuple-element.171) | copy-start | bytes 1540
  62.7 9.2 %copy-start.87 = (f32[128]{0:T(128)}, f32[128]{0:T(128)S(1)}, u32[]{:S(2)}) copy-start(f32[128]{0:T(128)S(1)} %get-tuple-element.172) | copy-start | bytes 1540
  62.8 9.2 %copy-start.89 = (f32[128]{0:T(128)}, f32[128]{0:T(128)S(1)}, u32[]{:S(2)}) copy-start(f32[128]{0:T(128)S(1)} %get-tuple-element.173) | copy-start | bytes 1540
  62.8 9.2 %copy-start.91 = (f32[128]{0:T(128)}, f32[128]{0:T(128)S(1)}, u32[]{:S(2)}) copy-start(f32[128]{0:T(128)S(1)} %get-tuple-element.174) | copy-start | bytes 1540
  62.8 9.2 %copy-start.93 = (f32[128]{0:T(128)}, f32[128]{0:T(128)S(1)}, u32[]{:S(2)}) copy-start(f32[128]{0:T(128)S(1)} %get-tuple-element.175) | copy-start | bytes 1540
  81.6 13.0 %all-to-all-start.3 = ((bf16[8,1,64,128]{3,2,1,0:T(8,128)(2,1)}), bf16[8,1,64,128]{3,2,1,0:T(8,128)(2,1)S(1)}, u32[]{:S(2)}, u32[]{:S(2)}) async-start(bf16[8,1,64,128]{3,2,1,0:T(8,128)(2,1)} %constant_dynamic-update-slice_fusion.8), calls=%async_computation.3 | async-start | bytes 262144 | tf_op jit(solution)/shard_map/all_to_all | solution.py:63
  94.6 12.7 %all-to-all-start.6 = ((bf16[8,2,4096]{2,1,0:T(2,128)(2,1)}), bf16[8,2,4096]{2,1,0:T(2,128)(2,1)S(1)}, u32[]{:S(2)}, u32[]{:S(2)}) async-start(bf16[8,2,4096]{2,1,0:T(2,128)(2,1)} %reshape.874), calls=%async_computation.6 | async-start | bytes 262144 | tf_op jit(solution)/shard_map/all_to_all | solution.py:56
  107.3 13.7 %all-to-all-start.4 = ((bf16[8,2,4096]{2,1,0:T(2,128)(2,1)}), bf16[8,2,4096]{2,1,0:T(2,128)(2,1)}, u32[]{:S(2)}, u32[]{:S(2)}) async-start(bf16[8,2,4096]{2,1,0:T(2,128)(2,1)} %reshape.872), calls=%async_computation.4 | async-start | bytes 262144 | tf_op jit(solution)/shard_map/all_to_all | solution.py:56
  137.8 5.3 copy-start.27
  145.6 15.8 %all-to-all-start.5 = ((bf16[8,1,64,128]{3,2,1,0:T(8,128)(2,1)}), bf16[8,1,64,128]{3,2,1,0:T(8,128)(2,1)}, u32[]{:S(2)}, u32[]{:S(2)}) async-start(bf16[8,1,64,128]{3,2,1,0:T(8,128)(2,1)} %constant_dynamic-update-slice_fusion.16), calls=%async_computation.5 | async-start | bytes 262144 | tf_op jit(solution)/shard_map/all_to_all | solution.py:63
  161.4 15.3 %all-to-all-start.7 = ((bf16[8,1,64,128]{3,2,1,0:T(8,128)(2,1)}), bf16[8,1,64,128]{3,2,1,0:T(8,128)(2,1)S(1)}, u32[]{:S(2)}, u32[]{:S(2)}) async-start(bf16[8,1,64,128]{3,2,1,0:T(8,128)(2,1)} %constant_dynamic-update-slice_fusion.24), calls=%async_computation.7 | async-start | bytes 262144 | tf_op jit(solution)/shard_map/all_to_all | solution.py:63
  207.9 5.3 copy-start.124
  207.9 5.3 copy-start.125
  207.9 5.3 copy-start.126
  208.0 5.3 copy-start.127
  208.6 12.8 %all-to-all-start.9 = ((bf16[8,1,64,128]{3,2,1,0:T(8,128)(2,1)}), bf16[8,1,64,128]{3,2,1,0:T(8,128)(2,1)S(1)}, u32[]{:S(2)}, u32[]{:S(2)}) async-start(bf16[8,1,64,128]{3,2,1,0:T(8,128)(2,1)} %constant_dynamic-update-slice_fusion.32), calls=%async_computation.9 | async-start | bytes 262144 | tf_op jit(solution)/shard_map/all_to_all | solution.py:63
  225.2 13.0 %all-to-all-start.10 = ((bf16[8,2,4096]{2,1,0:T(2,128)(2,1)}), bf16[8,2,4096]{2,1,0:T(2,128)(2,1)S(1)}, u32[]{:S(2)}, u32[]{:S(2)}) async-start(bf16[8,2,4096]{2,1,0:T(2,128)(2,1)} %reshape.878), calls=%async_computation.10 | async-start | bytes 262144 | tf_op jit(solution)/shard_map/all_to_all | solution.py:56
  230.1 264.9 %all-reduce.87.cloned.1.call-start = ((), (), s32[]{:S(2)}) async-start(), calls=%async_computation.12 | async-start | bytes 393216 | tf_op jit(solution)/shard_map/psum | solution.py:172
  255.9 240.7 %all-to-all-start.11 = ((bf16[8,1,64,128]{3,2,1,0:T(8,128)(2,1)}), bf16[8,1,64,128]{3,2,1,0:T(8,128)(2,1)S(1)}, u32[]{:S(2)}, u32[]{:S(2)}) async-start(bf16[8,1,64,128]{3,2,1,0:T(8,128)(2,1)} %constant_dynamic-update-slice_fusion.40), calls=%async_computation.11 | async-start | bytes 262144 | tf_op jit(solution)/shard_map/all_to_all | solution.py:63
  (124 other events, 211.6 us)
Sparse Core Ops, SparseCore 0:
  246.3 248.6 all-reduce.86
